TPU v7x, 128 devices: a whole 4x4x4 slice. The times are simulated.
128 devices in a mesh: dp: 4 (over z), expert: 32 (over x, y, core).
Axes of the slice: x: 4, y: 4, z: 4, core: 2. Of those that a mesh axis runs over, the one named last changes fastest.
Arguments:
- grad_parts: bfloat16 [4, 128, 128, 2048], P('dp', 'expert'), may hold values from -6 to 6
- first_moment: float32 [128, 128, 2048], P('expert', None, 'dp'), may hold values from -4 to 4
- second_moment: float32 [128, 128, 2048], P('expert', None, 'dp'), may hold values from 0.05 to 2
- master_weight: float32 [128, 128, 2048], P('expert', None, 'dp'), may hold values from -6 to 6
- old_owner: int32 [104], replicated, may hold values from 0 to 25, as said below
- new_owner: int32 [104], replicated, may hold values from 0 to 31, as said below
Outputs:
- new_master: float32 [192, 128, 2048], P('expert', None, 'dp')
- new_first: float32 [192, 128, 2048], P('expert', None, 'dp')
- new_second: float32 [192, 128, 2048], P('expert', None, 'dp')
- new_params: bfloat16 [192, 128, 2048], P('expert')
Inputs may be any that keep to these rules, and one draw needn't show every extreme that they name: `old_owner`: tiles are owned by devices 0 to 25 of the expert axis, exactly 4 each; the other devices own none, and their slots of the old-layout arrays are never read. `new_owner`: each device owns at most 6 tiles and some own exactly 6; the tiles of one old owner go to different new owners.
All inputs are finite; a program needn't handle non-finite values.
Results may differ from a plain program's by a relative error of at most 0.0085.
Values may be sent and summed in bfloat16 or wider, within the bound.
No kernel may reach another device: no remote copies, remote signals or barrier semaphores. Data moves between devices by JAX's collectives and lax.ppermute only.
A program may use at most 128 MiB of HBM per device.

v0:
```python
import jax
import jax.numpy as jnp
from jax import lax
from jax.sharding import PartitionSpec as P


def slot_ranks(owner, count):
    matches = (owner[:, None] == jnp.arange(count, dtype=jnp.int32)[None, :]).astype(jnp.int32)
    before = jnp.cumsum(matches, axis=0) - matches
    return jnp.sum(before * matches, axis=1)


def adam_step(gradient, moment_one, moment_two, weight):
    moment_one = 0.9 * moment_one + 0.1 * gradient
    moment_two = 0.95 * moment_two + 0.05 * gradient * gradient
    update = moment_one / (1.0 - 0.9**50) / (jnp.sqrt(moment_two / (1.0 - 0.95**50)) + 1e-08)
    weight = weight - 0.05 * (update + 0.1 * weight)
    return (weight, moment_one, moment_two)


def shards(grad_parts, first_moment, second_moment, master_weight, old_owner, new_owner):
    peer_count = lax.axis_size("expert")
    device = lax.axis_index("expert")
    old_slots = first_moment.shape[0]
    new_slots = min(old_slots + old_slots // 2, peer_count - peer_count // 5)
    old_rank = slot_ranks(old_owner, peer_count)
    new_rank = slot_ranks(new_owner, peer_count)
    targets = jnp.arange(peer_count, dtype=jnp.int32)
    outgoing = (old_owner == device)[:, None] & (new_owner[:, None] == targets[None, :])
    send_has = jnp.sum(outgoing.astype(jnp.int32), axis=0) > 0
    send_slot = jnp.sum(jnp.where(outgoing, old_rank[:, None], 0), axis=0)
    slot_ids = jnp.arange(new_slots, dtype=jnp.int32)
    wanted = (new_owner == device)[:, None] & (new_rank[:, None] == slot_ids[None, :])
    recv_has = jnp.sum(wanted.astype(jnp.int32), axis=0) > 0
    recv_source = jnp.sum(jnp.where(wanted, old_owner[:, None], 0), axis=0)

    def to_peers(values):
        return jnp.where(send_has[:, None, None], values[send_slot], 0.0)

    def from_peers(values):
        return jnp.where(recv_has[:, None, None], values[recv_source], 0.0)

    summed = lax.psum_scatter(grad_parts[0], "dp", scatter_dimension=2, tiled=True).astype(
        jnp.float32
    )
    weight, moment_one, moment_two = adam_step(summed, first_moment, second_moment, master_weight)
    results = (
        lax.all_to_all(
            to_peers(weight).astype(jnp.bfloat16), "expert", split_axis=0, concat_axis=0, tiled=True
        ).astype(jnp.float32),
        lax.all_to_all(
            to_peers(moment_one).astype(jnp.bfloat16),
            "expert",
            split_axis=0,
            concat_axis=0,
            tiled=True,
        ).astype(jnp.float32),
        lax.all_to_all(
            to_peers(moment_two).astype(jnp.bfloat16),
            "expert",
            split_axis=0,
            concat_axis=0,
            tiled=True,
        ).astype(jnp.float32),
    )
    new_master = from_peers(results[0])
    new_first = from_peers(results[1])
    new_second = from_peers(results[2])
    new_params = lax.all_gather(new_master.astype(jnp.bfloat16), "dp", axis=2, tiled=True)
    return (new_master, new_first, new_second, new_params)


def solution(mesh):
    placed = (
        P("dp", "expert", None, None),
        P("expert", None, "dp"),
        P("expert", None, "dp"),
        P("expert", None, "dp"),
        P(),
        P(),
    )
    return jax.shard_map(
        shards,
        mesh=mesh,
        in_specs=placed,
        out_specs=(
            P("expert", None, "dp"),
            P("expert", None, "dp"),
            P("expert", None, "dp"),
            P("expert", None, None),
        ),
        check_vma=False,
    )
```

profile of v0, /device:TPU:1, one launch (start us, length us, event | category | flops | bytes accessed | tf_op | source)
XLA Modules:
  0.0 297.9 jit_solution(7554008019410971334)
XLA Ops:
  7.2 0.0 reduce-scatter.2.cloned.1.call-start
  7.2 0.7 reduce-scatter.2.cloned.1.call-update
  7.9 0.7 fusion.2
  8.6 0.1 reduce_window_sum.18
  8.8 0.7 fusion.4
  9.5 0.1 reduce_window_sum.17
  9.7 0.8 select_reduce_fusion.1
  10.5 0.7 broadcast_compare_fusion.2
  11.2 0.9 convert_reduce_fusion
  12.1 31.5 %reduce-scatter.2.cloned.1.call-done = bf16[4,128,512]{2,1,0:T(8,128)(2,1)} async-done(((bf16[4,128,2048]{2,1,0:T(8,128)(2,1)}), bf16[4,128,512]{2,1,0:T(8,128)(2,1)}) %reduce-scatter.2.cloned.1.call-update) | async-done | bytes 524304 | tf_op jit(solution)/shard_map/reduce_scatter | solution.py:43
  43.6 3.0 multiply_subtract_fusion
  46.6 2.8 gather_fusion
  49.3 2.7 gather_fusion.2
  52.1 2.8 gather_fusion.4
  54.9 7.9 %select_convert_fusion = (bf16[32,128,512]{2,1,0:T(8,128)(2,1)}, bf16[32,128,512]{2,1,0:T(8,128)(2,1)S(1)}, bf16[32,128,512]{2,1,0:T(8,128)(2,1)S(1)}) fusion(bf16[32,128,512]{2,1,0:T(8,128)(2,1)} %gather_fusion.4, pred[32]{0:T(512)(128)(4,1)S(1)} %broadcast_compare_fusion, bf16[32,128,512]{2,1,0:T(8,128)(2,1)} %gather_fusion.2, ...), kind=kLoop, calls=%fused_computation.6 | loop fusion | flops 6291456 | bytes 25165856 | tf_op jit(solution)/shard_map/convert_element_type | solution.py:59
  62.8 58.0 %all_to_all.15 = bf16[32,128,512]{2,1,0:T(8,128)(2,1)} all-to-all(bf16[32,128,512]{2,1,0:T(8,128)(2,1)S(1)} %get-tuple-element.20), channel_id=1, replica_groups=mesh['dp'=4,'expert'=32] {'expert'}, dimensions={0} | all-to-all | bytes 8388608 | tf_op jit(solution)/shard_map/all_to_all | solution.py:48
  120.7 54.5 %all_to_all.16 = bf16[32,128,512]{2,1,0:T(8,128)(2,1)} all-to-all(bf16[32,128,512]{2,1,0:T(8,128)(2,1)S(1)} %get-tuple-element.19), channel_id=1, replica_groups=mesh['dp'=4,'expert'=32] {'expert'}, dimensions={0} | all-to-all | bytes 8388608 | tf_op jit(solution)/shard_map/all_to_all | solution.py:51
  175.2 0.0 copy-start
  175.2 4.8 %all-to-all-start.2 = ((bf16[32,128,512]{2,1,0:T(8,128)(2,1)}), bf16[32,128,512]{2,1,0:T(8,128)(2,1)}, u32[]{:S(2)}, u32[]{:S(2)}) async-start(bf16[32,128,512]{2,1,0:T(8,128)(2,1)} %get-tuple-element.18), calls=%async_computation.3 | async-start | bytes 8388608 | tf_op jit(solution)/shard_map/all_to_all | solution.py:58
  180.0 0.0 all-gather.2.cloned.1.call-start
  180.0 0.0 copy-done
  180.0 0.1 convert_reduce_fusion.1
  180.2 6.6 %convert_element_type.42 = f32[32,128,512]{2,1,0:T(8,128)} convert(bf16[32,128,512]{2,1,0:T(8,128)(2,1)} %all_to_all.15) | non-fusion elementwise | flops 2097152 | bytes 12582912 | tf_op jit(solution)/shard_map/convert_element_type | solution.py:50
  186.8 4.0 %gather_fusion.1 = f32[6,128,512]{2,1,0:T(8,128)S(1)} fusion(f32[32,128,512]{2,1,0:T(8,128)} %convert_element_type.42, s32[1024]{0:T(1024)S(1)} %pad_clamp_fusion), kind=kCustom, calls=%fused_computation.1 | custom fusion | bytes 3145752 | tf_op jit(solution)/shard_map/gather | solution.py:41
  190.8 6.6 %convert_element_type.44 = f32[32,128,512]{2,1,0:T(8,128)} convert(bf16[32,128,512]{2,1,0:T(8,128)(2,1)} %all_to_all.16) | non-fusion elementwise | flops 2097152 | bytes 12582912 | tf_op jit(solution)/shard_map/convert_element_type | solution.py:57
  197.4 4.0 %gather_fusion.3 = f32[6,128,512]{2,1,0:T(8,128)S(1)} fusion(f32[32,128,512]{2,1,0:T(8,128)} %convert_element_type.44, s32[1024]{0:T(1024)S(1)} %pad_clamp_fusion), kind=kCustom, calls=%fused_computation.3 | custom fusion | bytes 3145752 | tf_op jit(solution)/shard_map/gather | solution.py:41
  201.4 30.8 %all-to-all-done.2 = bf16[32,128,512]{2,1,0:T(8,128)(2,1)} async-done(((bf16[32,128,512]{2,1,0:T(8,128)(2,1)}), bf16[32,128,512]{2,1,0:T(8,128)(2,1)}, u32[]{:S(2)}, u32[]{:S(2)}) %all-to-all-start.2) | async-done | bytes 4194336 | tf_op jit(solution)/shard_map/all_to_all | solution.py:58
  232.2 6.6 %convert_element_type.46 = f32[32,128,512]{2,1,0:T(8,128)} convert(bf16[32,128,512]{2,1,0:T(8,128)(2,1)} %all-to-all-done.2) | non-fusion elementwise | flops 2097152 | bytes 12582912 | tf_op jit(solution)/shard_map/convert_element_type | solution.py:64
  238.8 5.2 %gather_fusion.5 = f32[6,128,512]{2,1,0:T(8,128)} fusion(f32[32,128,512]{2,1,0:T(8,128)} %convert_element_type.46, s32[1024]{0:T(1024)S(1)} %pad_clamp_fusion), kind=kCustom, calls=%fused_computation.5 | custom fusion | bytes 3145752 | tf_op jit(solution)/shard_map/gather | solution.py:41
  243.9 4.1 %broadcast_select_fusion = (f32[6,128,512]{2,1,0:T(8,128)}, f32[6,128,512]{2,1,0:T(8,128)}, bf16[6,128,512]{2,1,0:T(8,128)(2,1)}, f32[6,128,512]{2,1,0:T(8,128)}) fusion(f32[6,128,512]{2,1,0:T(8,128)} %gather_fusion.5, pred[6]{0:T(512)(128)(4,1)S(1)} %broadcast_compare_fusion.1, f32[6,128,512]{2,1,0:T(8,128)S(1)} %gather_fusion.3, ...), kind=kLoop, calls=%fused_computation.14 | loop fusion | flops 1572864 | bytes 10223622 | tf_op jit(solution)/shard_map/jit(_where)/select_n | solution.py:41
  248.0 0.0 all-gather.2.cloned.1.call-update
  248.1 39.1 %all-gather.2.cloned.1.call-done = bf16[6,128,2048]{2,1,0:T(8,128)(2,1)} async-done(((bf16[6,128,512]{2,1,0:T(8,128)(2,1)}), bf16[6,128,2048]{2,1,0:T(8,128)(2,1)}) %all-gather.2.cloned.1.call-update) | async-done | bytes 3145744 | tf_op jit(solution)/shard_map/all_gather | solution.py:69
  287.1 4.0 %copy.11 = bf16[6,128,2048]{2,1,0:T(8,128)(2,1)} copy(bf16[6,128,2048]{2,1,0:T(8,128)(2,1)} %all-gather.2.cloned.1.call-done) | data formatting | bytes 6291456
  (6 shorter events, 0.0 us)
Async XLA Ops:
  7.2 36.4 %reduce-scatter.2.cloned.1.call-start = ((), (), s32[]{:S(2)}) async-start(), calls=%async_computation.4 | async-start | bytes 2621440 | tf_op jit(solution)/shard_map/reduce_scatter | solution.py:43
  175.2 4.8 %copy-start = (s32[104]{0:T(128)S(1)}, s32[104]{0:T(128)}, u32[]{:S(2)}) copy-start(s32[104]{0:T(128)} %param.10) | copy-start | bytes 1252
  175.2 57.0 %all-to-all-start.2 = ((bf16[32,128,512]{2,1,0:T(8,128)(2,1)}), bf16[32,128,512]{2,1,0:T(8,128)(2,1)}, u32[]{:S(2)}, u32[]{:S(2)}) async-start(bf16[32,128,512]{2,1,0:T(8,128)(2,1)} %get-tuple-element.18), calls=%async_computation.3 | async-start | bytes 8388608 | tf_op jit(solution)/shard_map/all_to_all | solution.py:58
  180.0 107.2 %all-gather.2.cloned.1.call-start = ((), (), s32[]{:S(2)}) async-start(), calls=%async_computation.5 | async-start | bytes 3932160 | tf_op jit(solution)/shard_map/all_gather | solution.py:69
Sparse Core Ops, SparseCore 0:
  10.4 33.1 reduce-scatter.1
  248.2 38.9 all-gather.1
where the time goes:
time: 299 us; the launch traced here: 298 us
  blocking collectives  112 us (37%)
  waiting for transfers between devices  102 us (34%)
  other arithmetic  39 us (13%)
  local copies, waits for them, and re-layouts  25.5 us (9%)
  between operations  14.1 us (5%)
  starting transfers between devices  4.85 us (2%)
    all_to_all x1, blocking collectives, shards(): lax.all_to_all(to_peers(weight).astype(jnp.bfloat16), 'expert', split_axi...  58 us
    all_to_all x1, blocking collectives, shards(): lax.all_to_all(to_peers(moment_one).astype(jnp.bfloat16), 'expert', split...  54.5 us
    all_gather x1, waiting for transfers between devices, shards(): lax.all_gather(new_master.astype(jnp.bfloat16), 'dp', axis=2, tiled=True)  39.1 us
    reduce_scatter x1, waiting for transfers between devices, shards(): lax.psum_scatter(grad_parts[0], 'dp', scatter_dimension=2, tiled=True)  31.5 us
    all_to_all x1, waiting for transfers between devices, shards(): lax.all_to_all(to_peers(moment_two).astype(jnp.bfloat16), 'expert', split...  30.8 us
    convert_element_type x3, other arithmetic, shards(): results = (lax.all_to_all(to_peers(weight).astype(jnp.bfloat16), 'expert'...  19.7 us
    gather x3, local copies, waits for them, and re-layouts, from_peers(): return jnp.where(recv_has[:, None, None], values[recv_source], 0.0)  13.2 us
    gather x3, local copies, waits for them, and re-layouts, to_peers(): return jnp.where(send_has[:, None, None], values[send_slot], 0.0)  8.3 us
  transfers between devices with their start and end apart: 3, of which 3 were waited for; matrix products, arithmetic and copies ran while one was open for 9% of the time, Pallas kernels for 0%

commit v1 on v0

--- a/solution.py
+++ b/solution.py
@@ -66,7 +66,12 @@
     new_master = from_peers(results[0])
     new_first = from_peers(results[1])
     new_second = from_peers(results[2])
-    new_params = lax.all_gather(new_master.astype(jnp.bfloat16), "dp", axis=2, tiled=True)
+    new_params = jnp.concatenate(
+        lax.all_to_all(
+            jnp.stack([new_master.astype(jnp.bfloat16)] * lax.axis_size("dp")), "dp", 0, 0
+        ),
+        axis=2,
+    )
     return (new_master, new_first, new_second, new_params)
 
 

time: 299 us -> 305 us (1.020)
  blocking collectives: 112 us -> 152 us
  waiting for transfers between devices: 102 us -> 63 us
  local copies, waits for them, and re-layouts: 25.5 us -> 29.3 us
    all_to_all x0 -> x1, blocking collectives: none -> 39.1 us  [shards(): lax.all_to_all(jnp.stack([new_master.astype(jnp.bfloat16)] * lax.axis_siz...]
    all_gather x1 -> x0, waiting for transfers between devices: 39.1 us -> none  [shards(): lax.all_gather(new_master.astype(jnp.bfloat16), 'dp', axis=2, tiled=True)]
  transfers between devices with their start and end apart: 3 -> 2, of which waited for: 3 -> 2; matrix products, arithmetic and copies ran while one was open for 9% -> 8% of each run, Pallas kernels for 0% -> 0%
where the time goes in v1:
time: 305 us; the launch traced here: 302 us
  blocking collectives  152 us (50%)
  waiting for transfers between devices  63 us (21%)
  other arithmetic  38.7 us (13%)
  local copies, waits for them, and re-layouts  29.3 us (10%)
  between operations  14.1 us (5%)
  starting transfers between devices  4.81 us (2%)
    all_to_all x1, blocking collectives, shards(): lax.all_to_all(to_peers(weight).astype(jnp.bfloat16), 'expert', split_axi...  58 us
    all_to_all x1, blocking collectives, shards(): lax.all_to_all(to_peers(moment_one).astype(jnp.bfloat16), 'expert', split...  54.5 us
    all_to_all x1, blocking collectives, shards(): lax.all_to_all(jnp.stack([new_master.astype(jnp.bfloat16)] * lax.axis_siz...  39.1 us
    reduce_scatter x1, waiting for transfers between devices, shards(): lax.psum_scatter(grad_parts[0], 'dp', scatter_dimension=2, tiled=True)  31.5 us
    all_to_all x1, waiting for transfers between devices, shards(): lax.all_to_all(to_peers(moment_two).astype(jnp.bfloat16), 'expert', split...  30.9 us
    convert_element_type x3, other arithmetic, shards(): results = (lax.all_to_all(to_peers(weight).astype(jnp.bfloat16), 'expert'...  19.7 us
    gather x3, local copies, waits for them, and re-layouts, from_peers(): return jnp.where(recv_has[:, None, None], values[recv_source], 0.0)  13.2 us
    gather x3, local copies, waits for them, and re-layouts, to_peers(): return jnp.where(send_has[:, None, None], values[send_slot], 0.0)  8.3 us
  transfers between devices with their start and end apart: 2, of which 2 were waited for; matrix products, arithmetic and copies ran while one was open for 8% of the time, Pallas kernels for 0%

profile of v1, /device:TPU:1, one launch (start us, length us, event | category | flops | bytes accessed | tf_op | source)
XLA Modules:
  0.0 301.6 jit_solution(12725838400021941493)
XLA Ops:
  7.2 0.0 reduce-scatter.2.cloned.1.call-start
  7.2 0.7 reduce-scatter.2.cloned.1.call-update
  7.9 0.7 fusion.2
  8.6 0.1 reduce_window_sum.18
  8.8 0.7 fusion.4
  9.5 0.1 reduce_window_sum.17
  9.7 0.8 select_reduce_fusion.1
  10.5 0.7 broadcast_compare_fusion.2
  11.2 0.9 convert_reduce_fusion
  12.1 31.5 %reduce-scatter.2.cloned.1.call-done = bf16[4,128,512]{2,1,0:T(8,128)(2,1)} async-done(((bf16[4,128,2048]{2,1,0:T(8,128)(2,1)}), bf16[4,128,512]{2,1,0:T(8,128)(2,1)}) %reduce-scatter.2.cloned.1.call-update) | async-done | bytes 524304 | tf_op jit(solution)/shard_map/reduce_scatter | solution.py:43
  43.6 3.0 multiply_subtract_fusion
  46.6 2.8 gather_fusion
  49.3 2.7 gather_fusion.2
  52.1 2.8 gather_fusion.4
  54.9 7.9 %select_convert_fusion = (bf16[32,128,512]{2,1,0:T(8,128)(2,1)}, bf16[32,128,512]{2,1,0:T(8,128)(2,1)S(1)}, bf16[32,128,512]{2,1,0:T(8,128)(2,1)S(1)}) fusion(bf16[32,128,512]{2,1,0:T(8,128)(2,1)} %gather_fusion.4, pred[32]{0:T(512)(128)(4,1)S(1)} %broadcast_compare_fusion, bf16[32,128,512]{2,1,0:T(8,128)(2,1)} %gather_fusion.2, ...), kind=kLoop, calls=%fused_computation.6 | loop fusion | flops 6291456 | bytes 25165856 | tf_op jit(solution)/shard_map/convert_element_type | solution.py:59
  62.8 58.0 %all_to_all.20 = bf16[32,128,512]{2,1,0:T(8,128)(2,1)} all-to-all(bf16[32,128,512]{2,1,0:T(8,128)(2,1)S(1)} %get-tuple-element.28), channel_id=1, replica_groups=mesh['dp'=4,'expert'=32] {'expert'}, dimensions={0} | all-to-all | bytes 8388608 | tf_op jit(solution)/shard_map/all_to_all | solution.py:48
  120.7 54.5 %all_to_all.21 = bf16[32,128,512]{2,1,0:T(8,128)(2,1)} all-to-all(bf16[32,128,512]{2,1,0:T(8,128)(2,1)S(1)} %get-tuple-element.27), channel_id=1, replica_groups=mesh['dp'=4,'expert'=32] {'expert'}, dimensions={0} | all-to-all | bytes 8388608 | tf_op jit(solution)/shard_map/all_to_all | solution.py:51
  175.2 0.0 copy-start
  175.2 4.8 %all-to-all-start.2 = ((bf16[32,128,512]{2,1,0:T(8,128)(2,1)}), bf16[32,128,512]{2,1,0:T(8,128)(2,1)}, u32[]{:S(2)}, u32[]{:S(2)}) async-start(bf16[32,128,512]{2,1,0:T(8,128)(2,1)} %get-tuple-element.26), calls=%async_computation.3 | async-start | bytes 8388608 | tf_op jit(solution)/shard_map/all_to_all | solution.py:58
  180.0 0.0 copy-done
  180.0 0.1 convert_reduce_fusion.1
  180.2 6.6 %convert_element_type.44 = f32[32,128,512]{2,1,0:T(8,128)} convert(bf16[32,128,512]{2,1,0:T(8,128)(2,1)} %all_to_all.20) | non-fusion elementwise | flops 2097152 | bytes 12582912 | tf_op jit(solution)/shard_map/convert_element_type | solution.py:50
  186.7 4.0 %gather_fusion.1 = f32[6,128,512]{2,1,0:T(8,128)S(1)} fusion(f32[32,128,512]{2,1,0:T(8,128)} %convert_element_type.44, s32[1024]{0:T(1024)S(1)} %pad_clamp_fusion), kind=kCustom, calls=%fused_computation.1 | custom fusion | bytes 3145752 | tf_op jit(solution)/shard_map/gather | solution.py:41
  190.8 6.6 %convert_element_type.46 = f32[32,128,512]{2,1,0:T(8,128)} convert(bf16[32,128,512]{2,1,0:T(8,128)(2,1)} %all_to_all.21) | non-fusion elementwise | flops 2097152 | bytes 12582912 | tf_op jit(solution)/shard_map/convert_element_type | solution.py:57
  197.3 4.0 %gather_fusion.3 = f32[6,128,512]{2,1,0:T(8,128)S(1)} fusion(f32[32,128,512]{2,1,0:T(8,128)} %convert_element_type.46, s32[1024]{0:T(1024)S(1)} %pad_clamp_fusion), kind=kCustom, calls=%fused_computation.3 | custom fusion | bytes 3145752 | tf_op jit(solution)/shard_map/gather | solution.py:41
  201.3 30.9 %all-to-all-done.2 = bf16[32,128,512]{2,1,0:T(8,128)(2,1)} async-done(((bf16[32,128,512]{2,1,0:T(8,128)(2,1)}), bf16[32,128,512]{2,1,0:T(8,128)(2,1)}, u32[]{:S(2)}, u32[]{:S(2)}) %all-to-all-start.2) | async-done | bytes 4194336 | tf_op jit(solution)/shard_map/all_to_all | solution.py:58
  232.2 6.6 %convert_element_type.48 = f32[32,128,512]{2,1,0:T(8,128)} convert(bf16[32,128,512]{2,1,0:T(8,128)(2,1)} %all-to-all-done.2) | non-fusion elementwise | flops 2097152 | bytes 12582912 | tf_op jit(solution)/shard_map/convert_element_type | solution.py:64
  238.8 5.2 %gather_fusion.5 = f32[6,128,512]{2,1,0:T(8,128)} fusion(f32[32,128,512]{2,1,0:T(8,128)} %convert_element_type.48, s32[1024]{0:T(1024)S(1)} %pad_clamp_fusion), kind=kCustom, calls=%fused_computation.5 | custom fusion | bytes 3145752 | tf_op jit(solution)/shard_map/gather | solution.py:41
  243.9 3.9 %broadcast_select_fusion = (f32[6,128,512]{2,1,0:T(8,128)}, f32[6,128,512]{2,1,0:T(8,128)}, bf16[6,128,512]{2,1,0:T(8,128)(2,1)S(1)}, f32[6,128,512]{2,1,0:T(8,128)}) fusion(f32[6,128,512]{2,1,0:T(8,128)} %gather_fusion.5, pred[6]{0:T(512)(128)(4,1)S(1)} %broadcast_compare_fusion.1, f32[6,128,512]{2,1,0:T(8,128)S(1)} %gather_fusion.3, ...), kind=kLoop, calls=%fused_computation.14 | loop fusion | flops 1572864 | bytes 10223622 | tf_op jit(solution)/shard_map/jit(_where)/select_n | solution.py:41
  247.8 0.3 stack.2
  248.1 39.1 %all_to_all.22 = bf16[4,6,128,512]{3,2,1,0:T(8,128)(2,1)S(1)} all-to-all(bf16[4,6,128,512]{3,2,1,0:T(8,128)(2,1)S(1)} %stack.2), channel_id=1, replica_groups=mesh['dp'=4,'expert'=32] {'dp'}, dimensions={0} | all-to-all | bytes 6291456 | tf_op jit(solution)/shard_map/all_to_all | solution.py:70
  287.3 2.8 copy.12
  290.1 4.6 %copy.13 = bf16[6,128,2048]{2,1,0:T(8,128)(2,1)} copy(bf16[6,128,2048]{1,2,0:T(8,128)(2,1)} %bitcast.12) | data formatting | bytes 6291456
  (6 shorter events, 0.0 us)
Async XLA Ops:
  7.2 36.4 %reduce-scatter.2.cloned.1.call-start = ((), (), s32[]{:S(2)}) async-start(), calls=%async_computation.5 | async-start | bytes 2621440 | tf_op jit(solution)/shard_map/reduce_scatter | solution.py:43
  175.2 4.8 %copy-start = (s32[104]{0:T(128)S(1)}, s32[104]{0:T(128)}, u32[]{:S(2)}) copy-start(s32[104]{0:T(128)} %param.10) | copy-start | bytes 1252
  175.2 57.0 %all-to-all-start.2 = ((bf16[32,128,512]{2,1,0:T(8,128)(2,1)}), bf16[32,128,512]{2,1,0:T(8,128)(2,1)}, u32[]{:S(2)}, u32[]{:S(2)}) async-start(bf16[32,128,512]{2,1,0:T(8,128)(2,1)} %get-tuple-element.26), calls=%async_computation.3 | async-start | bytes 8388608 | tf_op jit(solution)/shard_map/all_to_all | solution.py:58
Sparse Core Ops, SparseCore 0:
  10.4 33.1 reduce-scatter.1
